TPU v7x, 32 devices: a whole 2x2x4 slice. The times are simulated.
32 devices in a mesh: row: 8 (over y, x, core), col: 4 (over z).
Axes of the slice: x: 2, y: 2, z: 4, core: 2. Of those that a mesh axis runs over, the one named last changes fastest.
Arguments:
- descriptors: bfloat16 [32, 6144], P(None, ('row', 'col')), may hold values from -6 to 6
- densities: float32 [6144], P(('row', 'col')), may hold values from 0.25 to 4
- vectors: float32 [32, 6144], P(None, ('row', 'col')), may hold values from -6 to 6
Outputs:
- next_block: float32 [32, 6144], P(None, ('row', 'col'))
All inputs are finite; a program needn't handle non-finite values.
Results may differ from a plain program's by a relative error of at most 0.0036.
Values may be sent and summed in bfloat16 or wider, within the bound.
No kernel may reach another device: no remote copies, remote signals or barrier semaphores. Data moves between devices by JAX's collectives and lax.ppermute only.
A program may use at most 64 MiB of HBM per device.

v0:
```python
import math
import jax
import jax.numpy as jnp
from jax import lax
from jax.sharding import PartitionSpec as P

kernel_width = 8.0


def tile_terms(targets, target_norm, piece):
    piece_feat, piece_vals, piece_inv = piece
    piece_norm = jnp.sum(jnp.square(piece_feat.astype(jnp.float32)), axis=0)
    feature_dim, target_count = targets.shape
    span_rows = math.gcd(target_count, 512)
    block_count = target_count // span_rows
    blocks = targets.reshape(feature_dim, block_count, span_rows).transpose(1, 0, 2)
    norm_blocks = target_norm.reshape(block_count, span_rows)

    def tile_block(block_item):
        block_feat, block_norm = block_item
        inner_prod = lax.dot_general(
            block_feat, piece_feat, (((0,), (0,)), ((), ())), preferred_element_type=jnp.float32
        )
        kernel = jnp.exp(
            -(block_norm[:, None] + piece_norm[None, :] - 2.0 * inner_prod) / kernel_width
        ).astype(jnp.bfloat16)
        numerator = lax.dot_general(
            piece_vals, kernel, (((1,), (1,)), ((), ())), preferred_element_type=jnp.float32
        )
        degree = lax.dot_general(
            piece_inv, kernel, (((1,), (1,)), ((), ())), preferred_element_type=jnp.float32
        )
        return (numerator, degree)

    numerator, degree = lax.map(tile_block, (blocks, norm_blocks))
    numerator = numerator.transpose(1, 0, 2).reshape(piece_vals.shape[0], target_count)
    degree = degree.transpose(1, 0, 2).reshape(1, target_count)
    return (numerator, degree)


def accumulate(targets, vec_count):
    target_norm = jnp.sum(jnp.square(targets.astype(jnp.float32)), axis=0)

    def fold_piece(running, piece, start):
        numerator, degree = tile_terms(targets, target_norm, piece)
        return (numerator, degree)

    initial = (
        jnp.zeros((vec_count, targets.shape[1]), jnp.float32),
        jnp.zeros((1, targets.shape[1]), jnp.float32),
    )
    return (fold_piece, initial)


def per_device(descriptors, densities, vectors):
    highest = lax.Precision.HIGHEST
    vec_count = vectors.shape[0]
    weighted = (vectors / densities[None, :]).astype(jnp.bfloat16)
    inverse = (1.0 / densities).astype(jnp.bfloat16)[None, :]
    targets = lax.all_gather(descriptors, "col", axis=1, tiled=True)
    fold_piece, initial = accumulate(targets, vec_count)
    partial_value = fold_piece(
        initial,
        (
            lax.all_gather(descriptors, "row", axis=1, tiled=True),
            lax.all_gather(weighted, "row", axis=1, tiled=True),
            lax.all_gather(inverse, "row", axis=1, tiled=True),
        ),
        jnp.int32(0),
    )
    numerator, degree = (
        lax.psum_scatter(partial_value[0], "col", scatter_dimension=1, tiled=True),
        lax.psum_scatter(partial_value[1], "col", scatter_dimension=1, tiled=True),
    )
    diffused = numerator / degree
    samples_float = float(descriptors.shape[1] * lax.axis_size("row") * lax.axis_size("col"))
    coupling, diffused_gram, basis_gram = lax.psum(
        (
            jnp.dot(vectors, diffused.T, precision=highest),
            jnp.dot(diffused, diffused.T, precision=highest),
            jnp.dot(vectors, vectors.T, precision=highest),
        ),
        ("row", "col"),
    )
    remainder = diffused - jnp.dot(coupling.T, vectors, precision=highest) / samples_float
    cross_term = jnp.dot(coupling.T, coupling, precision=highest)
    basis_term = jnp.dot(
        coupling.T, jnp.dot(basis_gram, coupling, precision=highest), precision=highest
    )
    spread = (
        diffused_gram
        - 2.0 * cross_term / samples_float
        + basis_term / (samples_float * samples_float)
    )
    factor = jnp.linalg.cholesky(spread)
    solved = jax.scipy.linalg.solve_triangular(factor, remainder, lower=True)
    return math.sqrt(samples_float) * solved


def solution(mesh):
    return jax.shard_map(
        per_device,
        mesh=mesh,
        in_specs=(P(None, ("row", "col")), P(("row", "col")), P(None, ("row", "col"))),
        out_specs=P(None, ("row", "col")),
        check_vma=False,
    )
```

profile of v0, /device:TPU:0, one launch (start us, length us, event | category | flops | bytes accessed | tf_op | source)
XLA Modules:
  0.0 157.3 jit_solution(3891402411580507994)
XLA Ops:
  6.5 11.0 %all-gather.2 = bf16[8,192,32]{1,2,0:T(8,128)(2,1)S(1)} all-gather(bf16[1,192,32]{1,2,0:T(8,128)(2,1)} %bitcast.102), channel_id=1, replica_groups=mesh['row'=8,'col'=4] {'row'}, dimensions={0}, use_global_device_ids=true | all-gather | bytes 110592 | tf_op jit(solution)/shard_map/all_gather | solution.py:65
  17.5 13.6 %all-gather.1 = bf16[4,192,32]{1,2,0:T(8,128)(2,1)S(1)} all-gather(bf16[1,192,32]{1,2,0:T(8,128)(2,1)} %bitcast.103), channel_id=1, replica_groups=mesh['row'=8,'col'=4] {'col'}, dimensions={0}, use_global_device_ids=true | all-gather | bytes 61440 | tf_op jit(solution)/shard_map/all_gather | solution.py:60
  31.7 9.0 %all-gather.3 = bf16[8,192,32]{1,2,0:T(8,128)(2,1)S(1)} all-gather(bf16[1,192,32]{1,2,0:T(8,128)(2,1)S(1)} %fusion.17), channel_id=1, replica_groups=mesh['row'=8,'col'=4] {'row'}, dimensions={0}, use_global_device_ids=true | all-gather | bytes 110592 | tf_op jit(solution)/shard_map/all_gather | solution.py:66
  40.9 0.6 dynamic-slice
  42.2 0.2 dynamic-update-slice.3
  42.4 13.2 %all-reduce = bf16[1536]{0:T(1024)(128)(2,1)S(1)} all-reduce(bf16[1536]{0:T(1024)(128)(2,1)S(1)} %dynamic-update-slice.3), channel_id=2, replica_groups=mesh['row'=8,'col'=4] {'row'}, use_global_device_ids=true, to_apply=%add | all-reduce | flops 1536 | bytes 6144
  55.6 3.6 %while.12 = (s32[]{:T(128)}, f32[3,32,256]{2,1,0:T(8,128)S(1)}, f32[3,1,256]{2,1,0:T(1,128)S(1)}, f32[3,256]{1,0:T(4,128)S(1)}, f32[1536]{0:T(1024)S(1)}, /*inde...) while((s32[]{:T(128)}, f32[3,32,256]{2,1,0:T(8,128)S(1)}, ...), condition=%wide.region_3.4_spmd, body=%wide.region_2.3_spmd.sunk | while | flops 53477376 | bytes 2623605 | solution.py:35
  55.7 0.5 fusion.52
  56.2 0.3 fusion.53
  56.5 0.3 fusion.54
  56.8 0.6 fusion.52
  57.4 0.3 fusion.53
  57.7 0.3 fusion.54
  58.0 0.6 fusion.52
  58.6 0.3 fusion.53
  58.9 0.3 fusion.54
  59.2 1.0 copy.40
  60.3 0.9 copy.42
  61.2 0.2 fusion.19
  61.4 19.1 %reduce-scatter.9.cloned.1.call-done = f32[192,1]{1,0:T(8,128)} async-done(((f32[768,1]{1,0:T(8,128)}), f32[192,1]{1,0:T(8,128)}) %reduce-scatter.9.cloned.1.call-update) | async-done | bytes 784
  80.4 1.0 copy.41
  81.4 20.4 %reduce-scatter.7.cloned.1.call-done = f32[192,32]{1,0:T(8,128)} async-done(((f32[768,32]{1,0:T(8,128)}), f32[192,32]{1,0:T(8,128)}) %reduce-scatter.7.cloned.1.call-update) | async-done | bytes 24592
  101.8 1.0 copy.39
  102.8 0.2 fusion.18
  103.0 0.2 convolution_bitcast_fusion.2
  103.1 39.0 %all-reduce.1 = (f32[32,32]{0,1:T(8,128)S(1)}, f32[32,32]{0,1:T(8,128)S(1)}, f32[32,32]{1,0:T(8,128)S(1)}) all-reduce(f32[32,32]{0,1:T(8,128)S(1)} %convolution_bitcast_fusion.2, f32[32,32]{0,1:T(8,128)S(1)} %fusion.18, f32[32,32]{1,0:T(8,128)S(1)} %fusion.19), channel_id=1, replica_groups=mesh['row'=8,'col'=4] {'row','col'}, use_global_device_ids=true, to_apply=%region_7.8 | all-reduce | flops 3072 | bytes 24576 | tf_op jit(solution)/shard_map/psum | solution.py:77
  142.6 0.2 fusion.12
  142.9 2.9 %cholesky.16 = f32[32,32]{1,0:T(8,128)S(1)} custom-call(f32[32,32]{1,0:T(8,128)S(1)} %fusion.16), custom_call_target="Cholesky" | custom-call | tf_op jit(solution)/shard_map/jit(cholesky)/cholesky | solution.py:95
  145.8 0.6 compare_reduce_fusion
  146.5 0.7 fusion.14
  147.1 2.4 %custom-call.7 = f32[1,32,32]{1,2,0:T(8,128)S(1)} custom-call(f32[1,32,32]{2,1,0:T(8,128)S(1)} %fusion.14), custom_call_target="InvertDiagBlocksLowerTriangular" | custom-call | tf_op jit(solution)/shard_map/jit(_solve_triangular)/triangular_solve | solution.py:96
  149.6 0.9 convolution_multiply_fusion.1
  (36 shorter events, 1.4 us)
Async XLA Ops:
  6.5 25.1 %copy-start.1 = (f32[192]{0:T(256)S(1)}, f32[192]{0:T(256)}, u32[]{:S(2)}) copy-start(f32[192]{0:T(256)} %param.6) | copy-start | bytes 2308
  6.5 25.1 %copy-start = (f32[32,192]{1,0:T(8,128)S(1)}, f32[32,192]{1,0:T(8,128)}, u32[]{:S(2)}) copy-start(f32[32,192]{1,0:T(8,128)} %param.7) | copy-start | bytes 73732
  6.5 73.9 %reduce-scatter.9.cloned.1.call-start = ((), (), s32[]{:S(2)}) async-start(), calls=%async_computation.3 | async-start | bytes 491520
  31.2 9.8 %copy-start.2 = (u32[32]{0:T(128)S(1)}, u32[32]{0:T(128)}, u32[]{:S(2)}) copy-start(u32[32]{0:T(128)} %constant.83) | copy-start | bytes 388
  60.2 41.6 %reduce-scatter.7.cloned.1.call-start = ((), (), s32[]{:S(2)}) async-start(), calls=%async_computation.2 | async-start | bytes 491520
Sparse Core Ops, SparseCore 0:
  60.3 20.0 reduce-scatter.8
  82.7 19.0 reduce-scatter.6
where the time goes:
time: 158 us; the launch traced here: 157 us
  blocking collectives  85.7 us (54%)
  waiting for transfers between devices  39.5 us (25%)
  between operations  14.2 us (9%)
  other arithmetic  6.76 us (4%)
  matrix products  5.55 us (4%)
  local copies, waits for them, and re-layouts  5.41 us (3%)
    unnamed x4, waiting for transfers between devices  39.5 us
    psum x1, blocking collectives, per_device(): lax.psum((jnp.dot(vectors, diffused.T, precision=highest), jnp.dot(diffus...  39 us
    all_gather x1, blocking collectives, per_device(): targets = lax.all_gather(descriptors, 'col', axis=1, tiled=True)  13.6 us
    unnamed x1, blocking collectives  13.2 us
    all_gather x1, blocking collectives, per_device(): lax.all_gather(descriptors, 'row', axis=1, tiled=True)  11 us
    all_gather x1, blocking collectives, per_device(): lax.all_gather(weighted, 'row', axis=1, tiled=True)  9.01 us
    unnamed x16, local copies, waits for them, and re-layouts  5.06 us
    another operation x3, other arithmetic, per_device(): factor = jnp.linalg.cholesky(spread)  3.6 us
  transfers between devices with their start and end apart: 2, of which 2 were waited for; matrix products, arithmetic and copies ran while one was open for 1% of the time, Pallas kernels for 0%

commit v1 on v0

--- a/solution.py
+++ b/solution.py
@@ -57,7 +57,12 @@
     vec_count = vectors.shape[0]
     weighted = (vectors / densities[None, :]).astype(jnp.bfloat16)
     inverse = (1.0 / densities).astype(jnp.bfloat16)[None, :]
-    targets = lax.all_gather(descriptors, "col", axis=1, tiled=True)
+    ring = [descriptors]
+    for hop in range(3):
+        ring.append(lax.ppermute(ring[-1], "col", [(dev, (dev + 1) % 4) for dev in range(4)]))
+    targets = jnp.roll(
+        jnp.concatenate(ring[::-1], axis=1), (lax.axis_index("col") + 1) * ring[0].shape[1], axis=1
+    )
     fold_piece, initial = accumulate(targets, vec_count)
     partial_value = fold_piece(
         initial,

time: 158 us -> 150 us (0.949)
  blocking collectives: 85.7 us -> 70.2 us
  starting transfers between devices: 0.04 us -> 6.35 us
    all_gather x1 -> x0, blocking collectives: 13.6 us -> none  [per_device(): targets = lax.all_gather(descriptors, 'col', axis=1, tiled=True)]
    ppermute x0 -> x3, starting transfers between devices: none -> 6.31 us  [per_device(): lax.ppermute(ring[-1], 'col', [(dev, (dev + 1) % 4) for dev in range(4)])]
    all_gather x1, blocking collectives: 11 us -> 9.38 us  [per_device(): lax.all_gather(descriptors, 'row', axis=1, tiled=True)]
    unnamed x16 -> x15, local copies, waits for them, and re-layouts: 5.06 us -> 5.03 us
  transfers between devices with their start and end apart: 2 -> 5, of which waited for: 2 -> 2; matrix products, arithmetic and copies ran while one was open for 1% -> 3% of each run, Pallas kernels for 0% -> 0%
where the time goes in v1:
time: 150 us; the launch traced here: 149 us
  blocking collectives  70.2 us (47%)
  waiting for transfers between devices  39.1 us (26%)
  between operations  14.3 us (10%)
  other arithmetic  8.28 us (6%)
  starting transfers between devices  6.35 us (4%)
  matrix products  5.55 us (4%)
  local copies, waits for them, and re-layouts  5.43 us (4%)
    unnamed x4, waiting for transfers between devices  39.1 us
    psum x1, blocking collectives, per_device(): lax.psum((jnp.dot(vectors, diffused.T, precision=highest), jnp.dot(diffus...  38.9 us
    unnamed x1, blocking collectives  12.9 us
    all_gather x1, blocking collectives, per_device(): lax.all_gather(descriptors, 'row', axis=1, tiled=True)  9.38 us
    all_gather x1, blocking collectives, per_device(): lax.all_gather(weighted, 'row', axis=1, tiled=True)  9.02 us
    ppermute x3, starting transfers between devices, per_device(): lax.ppermute(ring[-1], 'col', [(dev, (dev + 1) % 4) for dev in range(4)])  6.31 us
    unnamed x15, local copies, waits for them, and re-layouts  5.03 us
    another operation x3, other arithmetic, per_device(): factor = jnp.linalg.cholesky(spread)  3.6 us
  transfers between devices with their start and end apart: 5, of which 2 were waited for; matrix products, arithmetic and copies ran while one was open for 3% of the time, Pallas kernels for 0%

profile of v1, /device:TPU:0, one launch (start us, length us, event | category | flops | bytes accessed | tf_op | source)
XLA Modules:
  0.0 149.3 jit_solution(5756020107649181584)
XLA Ops:
  6.5 3.1 %collective-permute-start = (bf16[32,192]{1,0:T(8,128)(2,1)}, bf16[32,192]{1,0:T(8,128)(2,1)S(1)}, u32[]{:S(2)}, u32[]{:S(2)}) collective-permute-start(bf16[32,192]{1,0:T(8,128)(2,1)} %param.5), channel_id=1, source_target_pairs={{0,1},{1,2},{2,3},{3,0},{4,5},{5,6},{6,7},{7,4},{8,9},{9,10},{10,1... | collective-permute-start | bytes 36872 | tf_op jit(solution)/shard_map/ppermute | solution.py:62
  9.6 0.7 divide_convert_fusion.1
  10.3 0.8 fusion.17
  11.0 9.4 %all-gather.1 = bf16[8,192,32]{1,2,0:T(8,128)(2,1)S(1)} all-gather(bf16[1,192,32]{1,2,0:T(8,128)(2,1)} %bitcast.94), channel_id=1, replica_groups=mesh['row'=8,'col'=4] {'row'}, dimensions={0}, use_global_device_ids=true | all-gather | bytes 110592 | tf_op jit(solution)/shard_map/all_gather | solution.py:70
  20.7 1.6 %collective-permute-start.1 = (bf16[32,192]{1,0:T(8,128)(2,1)S(1)}, bf16[32,192]{1,0:T(8,128)(2,1)S(1)}, u32[]{:S(2)}, u32[]{:S(2)}) collective-permute-start(bf16[32,192]{1,0:T(8,128)(2,1)S(1)} %collective-permute-done), channel_id=1, source_target_pairs={{0,1},{1,2},{2,3},{3,0},{4,5},{5,6},{6,7},{7,4},{8,9},{9,10},{10,1... | collective-permute-start | bytes 36872 | tf_op jit(solution)/shard_map/ppermute | solution.py:62
  22.4 0.7 dynamic-slice
  23.8 0.2 dynamic-update-slice.3
  24.0 12.9 %all-reduce = bf16[1536]{0:T(1024)(128)(2,1)S(1)} all-reduce(bf16[1536]{0:T(1024)(128)(2,1)S(1)} %dynamic-update-slice.3), channel_id=2, replica_groups=mesh['row'=8,'col'=4] {'row'}, use_global_device_ids=true, to_apply=%add | all-reduce | flops 1536 | bytes 6144
  37.0 1.6 %collective-permute-start.2 = (bf16[32,192]{1,0:T(8,128)(2,1)S(1)}, bf16[32,192]{1,0:T(8,128)(2,1)S(1)}, u32[]{:S(2)}, u32[]{:S(2)}) collective-permute-start(bf16[32,192]{1,0:T(8,128)(2,1)S(1)} %collective-permute-done.1), channel_id=1, source_target_pairs={{0,1},{1,2},{2,3},{3,0},{4,5},{5,6},{6,7},{7,4},{8,9},{9,10},{10,1... | collective-permute-start | bytes 36872 | tf_op jit(solution)/shard_map/ppermute | solution.py:62
  38.6 9.0 %all-gather.2 = bf16[8,192,32]{1,2,0:T(8,128)(2,1)S(1)} all-gather(bf16[1,192,32]{1,2,0:T(8,128)(2,1)S(1)} %fusion.17), channel_id=1, replica_groups=mesh['row'=8,'col'=4] {'row'}, dimensions={0}, use_global_device_ids=true | all-gather | bytes 110592 | tf_op jit(solution)/shard_map/all_gather | solution.py:71
  48.1 3.6 %while.12 = (s32[]{:T(128)}, f32[3,32,256]{2,1,0:T(8,128)S(1)}, f32[3,1,256]{2,1,0:T(1,128)S(1)}, f32[3,256]{1,0:T(4,128)S(1)}, f32[1536]{0:T(1024)S(1)}, /*inde...) while((s32[]{:T(128)}, f32[3,32,256]{2,1,0:T(8,128)S(1)}, ...), condition=%wide.region_3.4_spmd, body=%wide.region_2.3_spmd.sunk | while | flops 53477376 | bytes 2623605 | solution.py:35
  48.2 0.5 fusion.52
  48.7 0.3 fusion.53
  49.0 0.3 fusion.54
  49.3 0.6 fusion.52
  49.9 0.3 fusion.53
  50.2 0.3 fusion.54
  50.5 0.6 fusion.52
  51.1 0.3 fusion.53
  51.4 0.3 fusion.54
  51.7 1.0 copy.37
  52.8 0.9 copy.39
  53.9 18.6 %reduce-scatter.9.cloned.1.call-done = f32[192,1]{1,0:T(8,128)} async-done(((f32[768,1]{1,0:T(8,128)}), f32[192,1]{1,0:T(8,128)}) %reduce-scatter.9.cloned.1.call-update) | async-done | bytes 784
  72.5 1.0 copy.38
  73.5 20.4 %reduce-scatter.7.cloned.1.call-done = f32[192,32]{1,0:T(8,128)} async-done(((f32[768,32]{1,0:T(8,128)}), f32[192,32]{1,0:T(8,128)}) %reduce-scatter.7.cloned.1.call-update) | async-done | bytes 24592
  93.9 1.0 copy.36
  95.2 38.9 %all-reduce.1 = (f32[32,32]{0,1:T(8,128)S(1)}, f32[32,32]{0,1:T(8,128)S(1)}, f32[32,32]{1,0:T(8,128)S(1)}) all-reduce(f32[32,32]{0,1:T(8,128)S(1)} %convolution_bitcast_fusion.2, f32[32,32]{0,1:T(8,128)S(1)} %fusion.18, f32[32,32]{1,0:T(8,128)S(1)} %fusion.19), channel_id=1, replica_groups=mesh['row'=8,'col'=4] {'row','col'}, use_global_device_ids=true, to_apply=%region_7.8 | all-reduce | flops 3072 | bytes 24576 | tf_op jit(solution)/shard_map/psum | solution.py:82
  134.9 2.9 %cholesky.16 = f32[32,32]{1,0:T(8,128)S(1)} custom-call(f32[32,32]{1,0:T(8,128)S(1)} %fusion.16), custom_call_target="Cholesky" | custom-call | tf_op jit(solution)/shard_map/jit(cholesky)/cholesky | solution.py:100
  137.9 0.6 compare_reduce_fusion
  138.5 0.7 fusion.14
  139.2 2.4 %custom-call.7 = f32[1,32,32]{1,2,0:T(8,128)S(1)} custom-call(f32[1,32,32]{2,1,0:T(8,128)S(1)} %fusion.14), custom_call_target="InvertDiagBlocksLowerTriangular" | custom-call | tf_op jit(solution)/shard_map/jit(_solve_triangular)/triangular_solve | solution.py:101
  141.6 0.9 convolution_multiply_fusion.1
  (40 shorter events, 2.1 us)
Async XLA Ops:
  6.5 15.9 %copy-start.2 = (u32[32]{0:T(128)S(1)}, u32[32]{0:T(128)}, u32[]{:S(2)}) copy-start(u32[32]{0:T(128)} %constant.109) | copy-start | bytes 388
  6.5 41.3 %copy-start.1 = (bf16[32,192]{1,0:T(8,128)(2,1)S(1)}, bf16[32,192]{1,0:T(8,128)(2,1)}, u32[]{:S(2)}) copy-start(bf16[32,192]{1,0:T(8,128)(2,1)} %param.5) | copy-start | bytes 36868
  6.5 66.0 %reduce-scatter.9.cloned.1.call-start = ((), (), s32[]{:S(2)}) async-start(), calls=%async_computation.3 | async-start | bytes 491520
  6.5 14.1 %collective-permute-start = (bf16[32,192]{1,0:T(8,128)(2,1)}, bf16[32,192]{1,0:T(8,128)(2,1)S(1)}, u32[]{:S(2)}, u32[]{:S(2)}) collective-permute-start(bf16[32,192]{1,0:T(8,128)(2,1)} %param.5), channel_id=1, source_target_pairs={{0,1},{1,2},{2,3},{3,0},{4,5},{5,6},{6,7},{7,4},{8,9},{9,10},{10,1... | collective-permute-start | bytes 36872 | tf_op jit(solution)/shard_map/ppermute | solution.py:62
  20.7 16.3 %collective-permute-start.1 = (bf16[32,192]{1,0:T(8,128)(2,1)S(1)}, bf16[32,192]{1,0:T(8,128)(2,1)S(1)}, u32[]{:S(2)}, u32[]{:S(2)}) collective-permute-start(bf16[32,192]{1,0:T(8,128)(2,1)S(1)} %collective-permute-done), channel_id=1, source_target_pairs={{0,1},{1,2},{2,3},{3,0},{4,5},{5,6},{6,7},{7,4},{8,9},{9,10},{10,1... | collective-permute-start | bytes 36872 | tf_op jit(solution)/shard_map/ppermute | solution.py:62
  37.0 10.9 %collective-permute-start.2 = (bf16[32,192]{1,0:T(8,128)(2,1)S(1)}, bf16[32,192]{1,0:T(8,128)(2,1)S(1)}, u32[]{:S(2)}, u32[]{:S(2)}) collective-permute-start(bf16[32,192]{1,0:T(8,128)(2,1)S(1)} %collective-permute-done.1), channel_id=1, source_target_pairs={{0,1},{1,2},{2,3},{3,0},{4,5},{5,6},{6,7},{7,4},{8,9},{9,10},{10,1... | collective-permute-start | bytes 36872 | tf_op jit(solution)/shard_map/ppermute | solution.py:62
  51.7 2.0 %copy-start = (f32[32,192]{1,0:T(8,128)S(1)}, f32[32,192]{1,0:T(8,128)}, u32[]{:S(2)}) copy-start(f32[32,192]{1,0:T(8,128)} %param.7) | copy-start | bytes 73732
  52.7 41.2 %reduce-scatter.7.cloned.1.call-start = ((), (), s32[]{:S(2)}) async-start(), calls=%async_computation.2 | async-start | bytes 491520
Sparse Core Ops, SparseCore 0:
  52.8 19.6 reduce-scatter.8
  74.8 19.0 reduce-scatter.6
